TPU v7x, 128 devices: a whole 4x4x4 slice. The times are simulated.
128 devices in a mesh: dom: 32 (over z, x, core), blk: 4 (over y).
Axes of the slice: x: 4, y: 4, z: 4, core: 2. Of those that a mesh axis runs over, the one named last changes fastest.
Arguments:
- displacement: float32 [16384, 96], P(('dom', 'blk')), may hold values from -6 to 6
- damage: float32 [16384, 96], P(('dom', 'blk')), may hold values from 0 to 0.95
- applied_load: float32 [16384, 96], P(('dom', 'blk')), may hold values from -300 to 300
- tangent: bfloat16 [16384, 5, 96, 96], P(('dom', 'blk')), may hold values from -0.625 to 0.625
- laplacian: bfloat16 [16384, 5, 96, 96], P(('dom', 'blk')), may hold values from -0.25 to 0.25
- block_columns: int32 [16384, 5], P(('dom', 'blk')), may hold values from 0 to 1023, as said below
- send_lists: int32 [32, 2, 256], P('dom'), may hold values from -1 to 511, as said below
- hist_mech: float32 [16384, 27, 96], P(('dom', 'blk')), may hold values from 0 to 200
- mech_dest: int32 [16384], P(('dom', 'blk')), may hold values from 0 to 16383, as said below
- strain_matrix: float32 [27, 96, 96], replicated, may hold values from -0.625 to 0.625
- quad_weight: float32 [27], replicated, may hold values from 0.018518519 to 0.055555556
Outputs:
- mech_out: float32 [16384, 96], P(('dom', 'blk'))
- dmg_out: float32 [16384, 96], P(('dom', 'blk'))
- norms: float32 [2], replicated
Inputs may be any that keep to these rules, and one draw needn't show every extreme that they name: mech_dest is a permutation of the block rows. The 128 rows of one device go to at most 2 rows of any one device (itself included), and that many are reached in every draw. `send_lists`: -1 marks an unused slot; used slots come first and name distinct rows of the group, numbered within the group. Group 0 lists nothing for the group below and the last group nothing for the group above. Some list uses all 256 slots. `block_columns`: entries of the ghost parts of the extended numbering name only used slots of the neighbours' lists, never those of a missing neighbour, and every used slot is named by some block row of the receiving group.
All inputs are finite; a program needn't handle non-finite values.
Results may differ from a plain program's by a relative error of at most 0.00047.
Values may be sent and summed in bfloat16 or wider, within the bound.
A program may use at most 128 MiB of HBM per device.

v0:
```python
import jax
import jax.numpy as jnp
from jax import lax
from jax.sharding import PartitionSpec as P


def padded(x, sides, width):
    for axis, dim in sides:
        peers, length = (lax.axis_size(axis), x.shape[dim])
        up = [(i, (i + 1) % peers) for i in range(peers - 1)]
        down = [(j, i) for i, j in up]
        last = lax.slice_in_dim(x, length - width, length, axis=dim)
        leading = lax.slice_in_dim(x, 0, width, axis=dim)
        before = lax.ppermute(last, axis, up)
        after = lax.ppermute(leading, axis, down)
        x = jnp.concatenate([before, x, after], axis=dim)
    return x


def on_device(
    displacement,
    damage,
    applied_load,
    tangent,
    laplacian,
    block_columns,
    send_lists,
    hist_mech,
    mech_dest,
    strain_matrix,
    quad_weight,
):
    row_count = displacement.shape[0]
    width = displacement.shape[1]
    devices = lax.axis_size(("dom", "blk"))
    capacity = row_count // devices + 1
    root_deg = jnp.sqrt((1.0 - damage) ** 2 + 0.001)
    fields = jnp.stack(
        [(root_deg * displacement).astype(jnp.bfloat16), damage.astype(jnp.bfloat16)]
    )
    group_fields = lax.all_gather(fields, "blk", axis=1, tiled=True)
    own_lists = send_lists[0]
    safe_index = jnp.maximum(own_lists, 0)
    picked = group_fields[:, safe_index]
    picked = jnp.where((own_lists >= 0)[None, :, :, None], picked, jnp.zeros((), jnp.bfloat16))
    framed = padded(picked, (("dom", 1),), 1)
    lower_ghost = framed[:, 0]
    upper_ghost = framed[:, 3]
    extended = jnp.concatenate([group_fields, lower_ghost, upper_ghost], axis=1)
    near_rows = extended[:, block_columns]
    mech_sum = jnp.einsum("ikrc,ikc->ir", tangent, near_rows[0], preferred_element_type=jnp.float32)
    diffuse = jnp.einsum(
        "ikrc,ikc->ir", laplacian, near_rows[1], preferred_element_type=jnp.float32
    )
    mech_res = root_deg * mech_sum - applied_load
    dest_device = mech_dest // row_count
    dest_slot = mech_dest % row_count
    dest_marks = (dest_device[:, None] == jnp.arange(devices, dtype=jnp.int32)[None, :]).astype(
        jnp.int32
    )
    slot_rank = jnp.sum(jnp.cumsum(dest_marks, axis=0) * dest_marks, axis=1) - 1
    bucket = dest_device * capacity + slot_rank
    slot_table = (
        jnp.full((devices * capacity,), -1, jnp.int32)
        .at[bucket]
        .set(dest_slot)
        .reshape(devices, capacity)
    )
    parcel = (
        jnp.zeros((devices * capacity,) + hist_mech.shape[1:], jnp.float32)
        .at[bucket]
        .set(hist_mech)
    )
    parcel = parcel.reshape((devices, capacity) + hist_mech.shape[1:])
    got_slots, got_rows = (
        lax.all_to_all(slot_table, ("dom", "blk"), split_axis=0, concat_axis=0, tiled=True),
        lax.all_to_all(parcel, ("dom", "blk"), split_axis=0, concat_axis=0, tiled=True),
    )
    target = jnp.where(got_slots >= 0, got_slots, row_count).reshape(-1)
    history = (
        jnp.zeros_like(hist_mech)
        .at[target]
        .set(got_rows.reshape((-1,) + hist_mech.shape[1:]), mode="drop")
    )
    strain = jnp.einsum("qcr,ir->iqc", strain_matrix, displacement, precision=lax.Precision.HIGHEST)
    energy = 0.5 * strain * strain
    source = jnp.einsum(
        "q,iqc->ic", quad_weight, jnp.maximum(history, energy), precision=lax.Precision.HIGHEST
    )
    dmg_res = diffuse + (1.0 + 2.0 * source) * damage - 2.0 * source
    totals = lax.psum((jnp.sum(mech_res * mech_res), jnp.sum(dmg_res * dmg_res)), ("dom", "blk"))
    entries = row_count * width * devices
    mech_norm = jnp.sqrt(totals[0] / entries + 1e-06)
    dmg_norm = jnp.sqrt(totals[1] / entries + 1e-06)
    return (mech_res / mech_norm, dmg_res / dmg_norm, jnp.stack([mech_norm, dmg_norm]))


def solution(mesh):
    in_specs = (
        P(("dom", "blk"), None),
        P(("dom", "blk"), None),
        P(("dom", "blk"), None),
        P(("dom", "blk"), None, None, None),
        P(("dom", "blk"), None, None, None),
        P(("dom", "blk"), None),
        P("dom", None, None),
        P(("dom", "blk"), None, None),
        P(("dom", "blk")),
        P(),
        P(),
    )
    out_specs = (P(("dom", "blk"), None), P(("dom", "blk"), None), P())
    return jax.shard_map(
        on_device, mesh=mesh, in_specs=in_specs, out_specs=out_specs, check_vma=False
    )
```

profile of v0, /device:TPU:1, one launch (start us, length us, event | category | flops | bytes accessed | tf_op | source)
XLA Modules:
  0.0 223.9 jit_solution(6956331945346940331)
XLA Ops:
  3.1 11.1 %all_gather.3 = bf16[2,512,96]{1,2,0:T(8,128)(2,1)S(1)} all-gather(bf16[2,128,96]{1,2,0:T(8,128)(2,1)S(1)} %pad_maximum_fusion.1), channel_id=1, replica_groups=mesh['dom'=32,'blk'=4] {'blk'}, dimensions={1}, use_global_device_ids=true | all-gather | bytes 245760 | tf_op jit(solution)/shard_map/all_gather | solution.py:41
  14.3 2.1 gather_fusion
  16.4 1.1 fusion.3
  17.5 0.9 fusion.11
  18.5 4.2 %collective-permute-start.1 = (bf16[2,1,256,96]{3,0,2,1:T(2,128)(2,1)}, bf16[2,1,256,96]{3,0,2,1:T(2,128)(2,1)}, u32[]{:S(2)}, u32[]{:S(2)}) collective-permute-start(bf16[2,1,256,96]{3,0,2,1:T(2,128)(2,1)} %get-tuple-element.13), channel_id=1, source_target_pairs={{4,0},{8,4},{12,8},{16,12},{20,16},{24,20},{28,24},{32,28},{36,32}... | collective-permute-start | bytes 294920 | tf_op jit(solution)/shard_map/ppermute | solution.py:15
  22.7 3.0 %collective-permute-start = (bf16[2,1,256,96]{3,0,2,1:T(2,128)(2,1)}, bf16[2,1,256,96]{3,0,2,1:T(2,128)(2,1)}, u32[]{:S(2)}, u32[]{:S(2)}) collective-permute-start(bf16[2,1,256,96]{3,0,2,1:T(2,128)(2,1)} %get-tuple-element.12), channel_id=1, source_target_pairs={{0,4},{4,8},{8,12},{12,16},{16,20},{20,24},{24,28},{28,32},{32,36}... | collective-permute-start | bytes 294920 | tf_op jit(solution)/shard_map/ppermute | solution.py:14
  26.2 1.0 scatter_custom_fusion
  27.9 9.0 %all-to-all-start = ((s32[128,1,2]{2,1,0:T(1,128)}), s32[128,1,2]{2,1,0:T(1,128)S(1)}, u32[]{:S(2)}, u32[]{:S(2)}) async-start(s32[128,1,2]{2,1,0:T(1,128)} %bitcast.20), calls=%async_computation | async-start | bytes 131072 | tf_op jit(solution)/shard_map/all_to_all | solution.py:76
  37.2 2.3 %copy.47 = f32[128,27,96]{2,1,0:T(8,128)S(1)} copy(f32[128,27,96]{0,2,1:T(8,128)} %param.18) | data formatting | bytes 2654208 | tf_op args[7]
  39.5 2.5 %broadcast_in_dim.44 = f32[256,27,96]{2,1,0:T(8,128)} broadcast(f32[]{:T(128)} %constant.30.clone.1), dimensions={} | broadcast | bytes 2654212 | tf_op jit(solution)/shard_map/broadcast_in_dim | solution.py:70
  42.0 15.7 %scatter_fusion = f32[256,27,96]{2,1,0:T(8,128)} fusion(f32[256,27,96]{2,1,0:T(8,128)} %broadcast_in_dim.44, s32[128]{0:T(128)S(1)} %compare_select_fusion.3, f32[128,27,96]{2,1,0:T(8,128)S(1)} %copy.47), kind=kCustom, calls=%fused_computation.3 | custom fusion | bytes 3981824 | tf_op jit(solution)/shard_map/scatter | solution.py:72
  57.7 7.4 %copy.49 = f32[128,2,27,96]{3,1,2,0:T(2,128)} copy(f32[128,2,27,96]{3,2,1,0:T(8,128)} %bitcast.49) | data formatting | bytes 5308416 | tf_op jit(solution)/shard_map/reshape | solution.py:74
  65.1 10.2 %all-to-all-start.1 = ((f32[128,2,27,96]{3,1,2,0:T(2,128)}), f32[128,2,27,96]{3,1,2,0:T(2,128)}, u32[]{:S(2)}, u32[]{:S(2)}) async-start(f32[128,2,27,96]{3,1,2,0:T(2,128)} %copy.49), calls=%async_computation.1 | async-start | bytes 7077888 | tf_op jit(solution)/shard_map/all_to_all | solution.py:77
  76.9 1.8 pad_maximum_fusion
  78.7 2.8 %gather_fusion.1 = bf16[640,2,96]{2,1,0:T(2,128)(2,1)S(1)} fusion(bf16[2,1024,96]{2,0,1:T(2,128)(2,1)S(1)} %pad_maximum_fusion, s32[1024]{0:T(1024)S(1)} %pad_clamp_fusion), kind=kCustom, calls=%fused_computation.1 | custom fusion | bytes 494080 | tf_op jit(solution)/shard_map/gather | solution.py:50
  82.4 11.1 %multiply_reduce_fusion = (f32[128,96]{0,1:T(8,128)S(1)}, f32[128,96]{0,1:T(8,128)S(1)}) fusion(f32[128,96,5]{0,1,2:T(8,128)S(1)} %bitcast_convert_fusion, bf16[128,5,96,96]{0,3,2,1:T(8,128)(2,1)} %param.15, bf16[128,5,96,96]{0,3,2,1:T(8,128)(2,1)} %param.14, f32[128,96,5]{0,1,2:T(8,128)S(1)} %bitcast_convert_fusion.1), kind=kLoop, calls=%fused_computation.5 | loop fusion | flops 35364864 | bytes 24182784 | tf_op jit(solution)/shard_map/ikrc,ikc->ir/dot_general | solution.py:52
  93.5 27.7 %all-to-all-done.1 = f32[128,2,27,96]{3,1,2,0:T(2,128)} async-done(((f32[128,2,27,96]{3,1,2,0:T(2,128)}), f32[128,2,27,96]{3,1,2,0:T(2,128)}, u32[]{:S(2)}, u32[]{:S(2)}) %all-to-all-start.1) | async-done | bytes 2654240 | tf_op jit(solution)/shard_map/all_to_all | solution.py:77
  121.2 3.9 %copy.50 = f32[128,2,27,96]{3,1,0,2:T(2,128)S(1)} copy(f32[128,2,27,96]{3,1,2,0:T(2,128)} %all-to-all-done.1) | data formatting | bytes 5308416 | tf_op jit(solution)/shard_map/all_to_all | solution.py:77
  125.2 4.0 %copy.51 = f32[256,27,96]{2,1,0:T(8,128)} copy(f32[256,27,96]{2,0,1:T(8,128)S(1)} %bitcast.50) | data formatting | bytes 5308416 | tf_op jit(solution)/shard_map/reshape | solution.py:83
  129.4 22.2 %scatter_fusion.1 = f32[128,27,96]{2,1,0:T(8,128)S(1)} fusion(f32[128,27,96]{2,1,0:T(8,128)S(1)} %broadcast_in_dim.40, s32[256]{0:T(256)S(1)} %bitcast.56, f32[256,27,96]{2,1,0:T(8,128)} %copy.51), kind=kCustom, calls=%fused_computation.4 | custom fusion | bytes 7963648 | tf_op jit(solution)/shard_map/scatter | solution.py:83
  151.7 1.8 copy.52
  153.5 2.6 %fusion.2 = f32[128,27,96]{0,2,1:T(8,128)S(1)} fusion(f32[128,27,96]{0,2,1:T(8,128)} %copy.52, f32[27,96,96]{2,1,0:T(8,128)S(1)} %copy-done, f32[128,96]{0,1:T(8,128)} %param.11), kind=kOutput, calls=%fused_computation.10 | convolution fusion | flops 383201280 | bytes 3698688 | tf_op jit(solution)/shard_map/qcr,ir->iqc/dot_general | solution.py:85
  156.1 1.8 fusion
  158.6 62.7 %all-reduce = (f32[]{:T(128)}, f32[]{:T(128)}) all-reduce(f32[]{:T(128)} %get-tuple-element.7, f32[]{:T(128)} %get-tuple-element.6), channel_id=1, replica_groups=mesh['dom'=32,'blk'=4] {'dom','blk'}, use_global_device_ids=true, to_apply=%region_1.2 | all-reduce | flops 2 | bytes 16 | tf_op jit(solution)/shard_map/psum | solution.py:91
  (49 shorter events, 8.6 us)
Async XLA Ops:
  0.6 152.8 %copy-start = (f32[27,96,96]{2,1,0:T(8,128)S(1)}, f32[27,96,96]{2,1,0:T(8,128)}, u32[]{:S(2)}) copy-start(f32[27,96,96]{2,1,0:T(8,128)} %param.20) | copy-start | bytes 2985988
  0.6 25.1 %copy-start.7 = (s32[128]{0:T(128)S(1)}, s32[128]{0:T(128)}, u32[]{:S(2)}) copy-start(s32[128]{0:T(128)} %param.19) | copy-start | bytes 1540
  0.7 36.2 %copy-start.5 = (s32[128,5]{0,1:T(8,128)S(1)}, s32[128,5]{0,1:T(8,128)}, u32[]{:S(2)}) copy-start(s32[128,5]{0,1:T(8,128)} %param.16) | copy-start | bytes 7684
  14.3 22.9 %copy-start.1 = (bf16[2,512,96]{2,0,1:T(2,128)(2,1)}, bf16[2,512,96]{2,0,1:T(2,128)(2,1)S(1)}, u32[]{:S(2)}) copy-start(bf16[2,512,96]{2,0,1:T(2,128)(2,1)S(1)} %copy.42) | copy-start | bytes 589828
  18.5 58.4 %collective-permute-start.1 = (bf16[2,1,256,96]{3,0,2,1:T(2,128)(2,1)}, bf16[2,1,256,96]{3,0,2,1:T(2,128)(2,1)}, u32[]{:S(2)}, u32[]{:S(2)}) collective-permute-start(bf16[2,1,256,96]{3,0,2,1:T(2,128)(2,1)} %get-tuple-element.13), channel_id=1, source_target_pairs={{4,0},{8,4},{12,8},{16,12},{20,16},{24,20},{28,24},{32,28},{36,32}... | collective-permute-start | bytes 294920 | tf_op jit(solution)/shard_map/ppermute | solution.py:15
  22.7 54.2 %collective-permute-start = (bf16[2,1,256,96]{3,0,2,1:T(2,128)(2,1)}, bf16[2,1,256,96]{3,0,2,1:T(2,128)(2,1)}, u32[]{:S(2)}, u32[]{:S(2)}) collective-permute-start(bf16[2,1,256,96]{3,0,2,1:T(2,128)(2,1)} %get-tuple-element.12), channel_id=1, source_target_pairs={{0,4},{4,8},{8,12},{12,16},{16,20},{20,24},{24,28},{28,32},{32,36}... | collective-permute-start | bytes 294920 | tf_op jit(solution)/shard_map/ppermute | solution.py:14
  27.9 37.2 %all-to-all-start = ((s32[128,1,2]{2,1,0:T(1,128)}), s32[128,1,2]{2,1,0:T(1,128)S(1)}, u32[]{:S(2)}, u32[]{:S(2)}) async-start(s32[128,1,2]{2,1,0:T(1,128)} %bitcast.20), calls=%async_computation | async-start | bytes 131072 | tf_op jit(solution)/shard_map/all_to_all | solution.py:76
  65.1 11.7 %copy-start.2 = (bf16[2,512,96]{2,0,1:T(2,128)(2,1)S(1)}, bf16[2,512,96]{2,0,1:T(2,128)(2,1)}, u32[]{:S(2)}) copy-start(bf16[2,512,96]{2,0,1:T(2,128)(2,1)} %copy-done.1) | copy-start | bytes 589828
  65.1 56.1 %all-to-all-start.1 = ((f32[128,2,27,96]{3,1,2,0:T(2,128)}), f32[128,2,27,96]{3,1,2,0:T(2,128)}, u32[]{:S(2)}, u32[]{:S(2)}) async-start(f32[128,2,27,96]{3,1,2,0:T(2,128)} %copy.49), calls=%async_computation.1 | async-start | bytes 7077888 | tf_op jit(solution)/shard_map/all_to_all | solution.py:77
  153.5 2.6 %copy-start.6 = (f32[27]{0:T(128)S(1)}, f32[27]{0:T(128)}, u32[]{:S(2)}) copy-start(f32[27]{0:T(128)} %param.21) | copy-start | bytes 328
  153.5 4.4 %copy-start.3 = (f32[128,96]{0,1:T(8,128)S(1)}, f32[128,96]{0,1:T(8,128)}, u32[]{:S(2)}) copy-start(f32[128,96]{0,1:T(8,128)} %param.12) | copy-start | bytes 147460
  153.5 4.4 %copy-start.4 = (f32[128,96]{0,1:T(8,128)S(1)}, f32[128,96]{0,1:T(8,128)}, u32[]{:S(2)}) copy-start(f32[128,96]{0,1:T(8,128)} %param.13) | copy-start | bytes 147460
where the time goes:
time: 226 us; the launch traced here: 224 us
  blocking collectives  73.8 us (33%)
  local copies, waits for them, and re-layouts  69.6 us (31%)
  waiting for transfers between devices  27.7 us (12%)
  starting transfers between devices  26.4 us (12%)
  other arithmetic  19.6 us (9%)
  matrix products  4.4 us (2%)
  between operations  2.38 us (1%)
    psum x1, blocking collectives, on_device(): lax.psum((jnp.sum(mech_res * mech_res), jnp.sum(dmg_res * dmg_res)), ('do...  62.7 us
    all_to_all x1, waiting for transfers between devices, on_device(): lax.all_to_all(parcel, ('dom', 'blk'), split_axis=0, concat_axis=0, tiled...  27.7 us
    scatter x2, local copies, waits for them, and re-layouts, on_device(): history = jnp.zeros_like(hist_mech).at[target].set(got_rows.reshape((-1,)...  24 us
    scatter x1, local copies, waits for them, and re-layouts, on_device(): parcel = jnp.zeros((devices * capacity,) + hist_mech.shape[1:], jnp.float...  15.7 us
    dot_general x1, other arithmetic, on_device(): jnp.einsum('ikrc,ikc->ir', laplacian, near_rows[1], preferred_element_typ...  11.1 us
    all_gather x1, blocking collectives, on_device(): group_fields = lax.all_gather(fields, 'blk', axis=1, tiled=True)  11.1 us
    all_to_all x1, starting transfers between devices, on_device(): lax.all_to_all(parcel, ('dom', 'blk'), split_axis=0, concat_axis=0, tiled...  10.2 us
    all_to_all x1, starting transfers between devices, on_device(): lax.all_to_all(slot_table, ('dom', 'blk'), split_axis=0, concat_axis=0, t...  8.96 us
  transfers between devices with their start and end apart: 4, of which 1 were waited for; matrix products, arithmetic and copies ran while one was open for 21% of the time, Pallas kernels for 0%

commit v1 on v0

--- a/solution.py
+++ b/solution.py
@@ -88,7 +88,9 @@
         "q,iqc->ic", quad_weight, jnp.maximum(history, energy), precision=lax.Precision.HIGHEST
     )
     dmg_res = diffuse + (1.0 + 2.0 * source) * damage - 2.0 * source
-    totals = lax.psum((jnp.sum(mech_res * mech_res), jnp.sum(dmg_res * dmg_res)), ("dom", "blk"))
+    totals = lax.psum(
+        lax.psum((jnp.sum(mech_res * mech_res), jnp.sum(dmg_res * dmg_res)), "dom"), "blk"
+    )
     entries = row_count * width * devices
     mech_norm = jnp.sqrt(totals[0] / entries + 1e-06)
     dmg_norm = jnp.sqrt(totals[1] / entries + 1e-06)

time: 226 us -> 235 us (1.040)
  blocking collectives: 73.8 us -> 81.9 us
    psum x1 -> x2, blocking collectives: 62.7 us -> 70.9 us  [the longest x1 62.5 us: on_device(): lax.psum((jnp.sum(mech_res * mech_res), jnp.sum(dmg_res * dmg_res)), 'dom')]
  transfers between devices with their start and end apart: 4 -> 4, of which waited for: 1 -> 1; matrix products, arithmetic and copies ran while one was open for 21% -> 20% of each run, Pallas kernels for 0% -> 0%
where the time goes in v1:
time: 235 us; the launch traced here: 232 us
  blocking collectives  81.9 us (35%)
  local copies, waits for them, and re-layouts  69.6 us (30%)
  waiting for transfers between devices  27.7 us (12%)
  starting transfers between devices  26.4 us (11%)
  other arithmetic  19.6 us (8%)
  matrix products  4.4 us (2%)
  between operations  2.38 us (1%)
    psum x1, blocking collectives, on_device(): lax.psum((jnp.sum(mech_res * mech_res), jnp.sum(dmg_res * dmg_res)), 'dom')  62.5 us
    all_to_all x1, waiting for transfers between devices, on_device(): lax.all_to_all(parcel, ('dom', 'blk'), split_axis=0, concat_axis=0, tiled...  27.7 us
    scatter x2, local copies, waits for them, and re-layouts, on_device(): history = jnp.zeros_like(hist_mech).at[target].set(got_rows.reshape((-1,)...  24 us
    scatter x1, local copies, waits for them, and re-layouts, on_device(): parcel = jnp.zeros((devices * capacity,) + hist_mech.shape[1:], jnp.float...  15.7 us
    dot_general x1, other arithmetic, on_device(): jnp.einsum('ikrc,ikc->ir', laplacian, near_rows[1], preferred_element_typ...  11.1 us
    all_gather x1, blocking collectives, on_device(): group_fields = lax.all_gather(fields, 'blk', axis=1, tiled=True)  11.1 us
    all_to_all x1, starting transfers between devices, on_device(): lax.all_to_all(parcel, ('dom', 'blk'), split_axis=0, concat_axis=0, tiled...  10.2 us
    all_to_all x1, starting transfers between devices, on_device(): lax.all_to_all(slot_table, ('dom', 'blk'), split_axis=0, concat_axis=0, t...  8.96 us
  transfers between devices with their start and end apart: 4, of which 1 were waited for; matrix products, arithmetic and copies ran while one was open for 20% of the time, Pallas kernels for 0%

profile of v1, /device:TPU:1, one launch (start us, length us, event | category | flops | bytes accessed | tf_op | source)
XLA Modules:
  0.0 232.1 jit_solution(13431532739425287816)
XLA Ops:
  3.1 11.1 %all_gather.3 = bf16[2,512,96]{1,2,0:T(8,128)(2,1)S(1)} all-gather(bf16[2,128,96]{1,2,0:T(8,128)(2,1)S(1)} %pad_maximum_fusion.1), channel_id=1, replica_groups=mesh['dom'=32,'blk'=4] {'blk'}, dimensions={1}, use_global_device_ids=true | all-gather | bytes 245760 | tf_op jit(solution)/shard_map/all_gather | solution.py:41
  14.3 2.1 gather_fusion
  16.4 1.1 fusion.3
  18.5 4.2 %collective-permute-start.1 = (bf16[2,1,256,96]{3,0,2,1:T(2,128)(2,1)}, bf16[2,1,256,96]{3,0,2,1:T(2,128)(2,1)}, u32[]{:S(2)}, u32[]{:S(2)}) collective-permute-start(bf16[2,1,256,96]{3,0,2,1:T(2,128)(2,1)} %get-tuple-element.15), channel_id=1, source_target_pairs={{4,0},{8,4},{12,8},{16,12},{20,16},{24,20},{28,24},{32,28},{36,32}... | collective-permute-start | bytes 294920 | tf_op jit(solution)/shard_map/ppermute | solution.py:15
  22.7 3.0 %collective-permute-start = (bf16[2,1,256,96]{3,0,2,1:T(2,128)(2,1)}, bf16[2,1,256,96]{3,0,2,1:T(2,128)(2,1)}, u32[]{:S(2)}, u32[]{:S(2)}) collective-permute-start(bf16[2,1,256,96]{3,0,2,1:T(2,128)(2,1)} %get-tuple-element.14), channel_id=1, source_target_pairs={{0,4},{4,8},{8,12},{12,16},{16,20},{20,24},{24,28},{28,32},{32,36}... | collective-permute-start | bytes 294920 | tf_op jit(solution)/shard_map/ppermute | solution.py:14
  26.2 1.0 scatter_custom_fusion
  27.9 9.0 %all-to-all-start = ((s32[128,1,2]{2,1,0:T(1,128)}), s32[128,1,2]{2,1,0:T(1,128)S(1)}, u32[]{:S(2)}, u32[]{:S(2)}) async-start(s32[128,1,2]{2,1,0:T(1,128)} %bitcast.20), calls=%async_computation | async-start | bytes 131072 | tf_op jit(solution)/shard_map/all_to_all | solution.py:76
  37.2 2.3 copy.47
  39.5 2.5 %broadcast_in_dim.44 = f32[256,27,96]{2,1,0:T(8,128)} broadcast(f32[]{:T(128)} %constant.30.clone.1), dimensions={} | broadcast | bytes 2654212 | tf_op jit(solution)/shard_map/broadcast_in_dim | solution.py:70
  42.0 15.7 %scatter_fusion = f32[256,27,96]{2,1,0:T(8,128)} fusion(f32[256,27,96]{2,1,0:T(8,128)} %broadcast_in_dim.44, s32[128]{0:T(128)S(1)} %compare_select_fusion.3, f32[128,27,96]{2,1,0:T(8,128)S(1)} %copy.47), kind=kCustom, calls=%fused_computation.3 | custom fusion | bytes 3981824 | tf_op jit(solution)/shard_map/scatter | solution.py:72
  57.7 7.4 %copy.49 = f32[128,2,27,96]{3,1,2,0:T(2,128)} copy(f32[128,2,27,96]{3,2,1,0:T(8,128)} %bitcast.49) | data formatting | bytes 5308416 | tf_op jit(solution)/shard_map/reshape | solution.py:74
  65.1 10.2 %all-to-all-start.1 = ((f32[128,2,27,96]{3,1,2,0:T(2,128)}), f32[128,2,27,96]{3,1,2,0:T(2,128)}, u32[]{:S(2)}, u32[]{:S(2)}) async-start(f32[128,2,27,96]{3,1,2,0:T(2,128)} %copy.49), calls=%async_computation.1 | async-start | bytes 7077888 | tf_op jit(solution)/shard_map/all_to_all | solution.py:77
  76.9 1.8 pad_maximum_fusion
  78.7 2.8 %gather_fusion.1 = bf16[640,2,96]{2,1,0:T(2,128)(2,1)S(1)} fusion(bf16[2,1024,96]{2,0,1:T(2,128)(2,1)S(1)} %pad_maximum_fusion, s32[1024]{0:T(1024)S(1)} %pad_clamp_fusion), kind=kCustom, calls=%fused_computation.1 | custom fusion | bytes 494080 | tf_op jit(solution)/shard_map/gather | solution.py:50
  82.4 11.1 %multiply_reduce_fusion = (f32[128,96]{0,1:T(8,128)S(1)}, f32[128,96]{0,1:T(8,128)S(1)}) fusion(f32[128,96,5]{0,1,2:T(8,128)S(1)} %bitcast_convert_fusion, bf16[128,5,96,96]{0,3,2,1:T(8,128)(2,1)} %param.15, bf16[128,5,96,96]{0,3,2,1:T(8,128)(2,1)} %param.14, f32[128,96,5]{0,1,2:T(8,128)S(1)} %bitcast_convert_fusion.1), kind=kLoop, calls=%fused_computation.5 | loop fusion | flops 35364864 | bytes 24182784 | tf_op jit(solution)/shard_map/ikrc,ikc->ir/dot_general | solution.py:52
  93.5 27.7 %all-to-all-done.1 = f32[128,2,27,96]{3,1,2,0:T(2,128)} async-done(((f32[128,2,27,96]{3,1,2,0:T(2,128)}), f32[128,2,27,96]{3,1,2,0:T(2,128)}, u32[]{:S(2)}, u32[]{:S(2)}) %all-to-all-start.1) | async-done | bytes 2654240 | tf_op jit(solution)/shard_map/all_to_all | solution.py:77
  121.2 3.9 %copy.50 = f32[128,2,27,96]{3,1,0,2:T(2,128)S(1)} copy(f32[128,2,27,96]{3,1,2,0:T(2,128)} %all-to-all-done.1) | data formatting | bytes 5308416 | tf_op jit(solution)/shard_map/all_to_all | solution.py:77
  125.2 4.0 %copy.51 = f32[256,27,96]{2,1,0:T(8,128)} copy(f32[256,27,96]{2,0,1:T(8,128)S(1)} %bitcast.50) | data formatting | bytes 5308416 | tf_op jit(solution)/shard_map/reshape | solution.py:83
  129.4 22.2 %scatter_fusion.1 = f32[128,27,96]{2,1,0:T(8,128)S(1)} fusion(f32[128,27,96]{2,1,0:T(8,128)S(1)} %broadcast_in_dim.40, s32[256]{0:T(256)S(1)} %bitcast.56, f32[256,27,96]{2,1,0:T(8,128)} %copy.51), kind=kCustom, calls=%fused_computation.4 | custom fusion | bytes 7963648 | tf_op jit(solution)/shard_map/scatter | solution.py:83
  151.7 1.8 copy.52
  153.5 2.6 %fusion.2 = f32[128,27,96]{0,2,1:T(8,128)S(1)} fusion(f32[128,27,96]{0,2,1:T(8,128)} %copy.52, f32[27,96,96]{2,1,0:T(8,128)S(1)} %copy-done, f32[128,96]{0,1:T(8,128)} %param.11), kind=kOutput, calls=%fused_computation.10 | convolution fusion | flops 383201280 | bytes 3698688 | tf_op jit(solution)/shard_map/qcr,ir->iqc/dot_general | solution.py:85
  156.1 1.8 fusion
  158.6 62.5 %all-reduce = (f32[]{:T(128)}, f32[]{:T(128)}) all-reduce(f32[]{:T(128)} %get-tuple-element.7, f32[]{:T(128)} %get-tuple-element.6), channel_id=1, replica_groups=mesh['dom'=32,'blk'=4] {'dom'}, use_global_device_ids=true, to_apply=%region_1.2 | all-reduce | flops 2 | bytes 16 | tf_op jit(solution)/shard_map/psum | solution.py:92
  221.1 8.3 %all-reduce.1 = (f32[]{:T(128)}, f32[]{:T(128)}) all-reduce(f32[]{:T(128)} %get-tuple-element.8, f32[]{:T(128)} %get-tuple-element.9), channel_id=1, replica_groups=mesh['dom'=32,'blk'=4] {'blk'}, use_global_device_ids=true, to_apply=%region_2.3 | all-reduce | flops 2 | bytes 16 | tf_op jit(solution)/shard_map/psum | solution.py:91
  (50 shorter events, 9.5 us)
Async XLA Ops:
  0.6 152.8 %copy-start = (f32[27,96,96]{2,1,0:T(8,128)S(1)}, f32[27,96,96]{2,1,0:T(8,128)}, u32[]{:S(2)}) copy-start(f32[27,96,96]{2,1,0:T(8,128)} %param.20) | copy-start | bytes 2985988
  0.6 25.1 %copy-start.7 = (s32[128]{0:T(128)S(1)}, s32[128]{0:T(128)}, u32[]{:S(2)}) copy-start(s32[128]{0:T(128)} %param.19) | copy-start | bytes 1540
  0.7 36.2 %copy-start.5 = (s32[128,5]{0,1:T(8,128)S(1)}, s32[128,5]{0,1:T(8,128)}, u32[]{:S(2)}) copy-start(s32[128,5]{0,1:T(8,128)} %param.16) | copy-start | bytes 7684
  14.3 22.9 %copy-start.1 = (bf16[2,512,96]{2,0,1:T(2,128)(2,1)}, bf16[2,512,96]{2,0,1:T(2,128)(2,1)S(1)}, u32[]{:S(2)}) copy-start(bf16[2,512,96]{2,0,1:T(2,128)(2,1)S(1)} %copy.42) | copy-start | bytes 589828
  18.5 58.4 %collective-permute-start.1 = (bf16[2,1,256,96]{3,0,2,1:T(2,128)(2,1)}, bf16[2,1,256,96]{3,0,2,1:T(2,128)(2,1)}, u32[]{:S(2)}, u32[]{:S(2)}) collective-permute-start(bf16[2,1,256,96]{3,0,2,1:T(2,128)(2,1)} %get-tuple-element.15), channel_id=1, source_target_pairs={{4,0},{8,4},{12,8},{16,12},{20,16},{24,20},{28,24},{32,28},{36,32}... | collective-permute-start | bytes 294920 | tf_op jit(solution)/shard_map/ppermute | solution.py:15
  22.7 54.2 %collective-permute-start = (bf16[2,1,256,96]{3,0,2,1:T(2,128)(2,1)}, bf16[2,1,256,96]{3,0,2,1:T(2,128)(2,1)}, u32[]{:S(2)}, u32[]{:S(2)}) collective-permute-start(bf16[2,1,256,96]{3,0,2,1:T(2,128)(2,1)} %get-tuple-element.14), channel_id=1, source_target_pairs={{0,4},{4,8},{8,12},{12,16},{16,20},{20,24},{24,28},{28,32},{32,36}... | collective-permute-start | bytes 294920 | tf_op jit(solution)/shard_map/ppermute | solution.py:14
  27.9 37.2 %all-to-all-start = ((s32[128,1,2]{2,1,0:T(1,128)}), s32[128,1,2]{2,1,0:T(1,128)S(1)}, u32[]{:S(2)}, u32[]{:S(2)}) async-start(s32[128,1,2]{2,1,0:T(1,128)} %bitcast.20), calls=%async_computation | async-start | bytes 131072 | tf_op jit(solution)/shard_map/all_to_all | solution.py:76
  65.1 11.7 %copy-start.2 = (bf16[2,512,96]{2,0,1:T(2,128)(2,1)S(1)}, bf16[2,512,96]{2,0,1:T(2,128)(2,1)}, u32[]{:S(2)}) copy-start(bf16[2,512,96]{2,0,1:T(2,128)(2,1)} %copy-done.1) | copy-start | bytes 589828
  65.1 56.1 %all-to-all-start.1 = ((f32[128,2,27,96]{3,1,2,0:T(2,128)}), f32[128,2,27,96]{3,1,2,0:T(2,128)}, u32[]{:S(2)}, u32[]{:S(2)}) async-start(f32[128,2,27,96]{3,1,2,0:T(2,128)} %copy.49), calls=%async_computation.1 | async-start | bytes 7077888 | tf_op jit(solution)/shard_map/all_to_all | solution.py:77
  153.5 2.6 %copy-start.6 = (f32[27]{0:T(128)S(1)}, f32[27]{0:T(128)}, u32[]{:S(2)}) copy-start(f32[27]{0:T(128)} %param.21) | copy-start | bytes 328
  153.5 4.4 %copy-start.3 = (f32[128,96]{0,1:T(8,128)S(1)}, f32[128,96]{0,1:T(8,128)}, u32[]{:S(2)}) copy-start(f32[128,96]{0,1:T(8,128)} %param.12) | copy-start | bytes 147460
  153.5 4.4 %copy-start.4 = (f32[128,96]{0,1:T(8,128)S(1)}, f32[128,96]{0,1:T(8,128)}, u32[]{:S(2)}) copy-start(f32[128,96]{0,1:T(8,128)} %param.13) | copy-start | bytes 147460
